TPU v7x, 128 devices: a whole 4x4x4 slice. The times are simulated.
128 devices in a mesh: grp: 4 (over z), slab: 32 (over y, x, core).
Axes of the slice: x: 4, y: 4, z: 4, core: 2. Of those that a mesh axis runs over, the one named last changes fastest.
Arguments:
- tensor: float32 [672, 256, 672], P('grp', 'slab'), may hold values from -20 to 20
- start_one: float32 [672, 96], replicated, may hold values from -6 to 6
- start_two: float32 [672, 96], replicated, may hold values from -6 to 6
Outputs:
- basis_one: float32 [672, 96], replicated
- basis_two: float32 [672, 96], replicated
- core: float32 [96, 256, 96], P('grp', 'slab')
All inputs are finite; a program needn't handle non-finite values.
Results may differ from a plain program's by a relative error of at most 0.0003.
Values sent between devices are 32-bit elements; how exact they have to be, the bound alone decides.
A program may use at most 64 MiB of HBM per device.

v0:
```python
import jax
import jax.numpy as jnp
from jax import lax
from jax.sharding import PartitionSpec as P

ITERS = 2
HIGH = lax.Precision.HIGHEST


def orthonormal(widened):
    cross = jnp.dot(widened.T, widened, precision=HIGH)
    lower_small = jnp.linalg.cholesky(cross)
    return lax.linalg.triangular_solve(
        lower_small, widened, left_side=False, lower=True, transpose_a=True
    )


def iterate_basis(gram, start):
    current = start
    for _ in range(ITERS):
        current = orthonormal(jnp.dot(gram, current, precision=HIGH))
    return current


def local(tensor, start_one, start_two):
    block_gram = jnp.einsum("jmi,jmk->ik", tensor, tensor, precision=HIGH)
    gram_one = lax.psum(block_gram, ("grp", "slab"))
    basis_one = iterate_basis(gram_one, start_one)
    reduced = jnp.einsum("jmi,ia->jma", tensor, basis_one, precision=HIGH)
    regrouped = lax.all_to_all(reduced, "grp", split_axis=1, concat_axis=0, tiled=True)
    block_second = jnp.einsum("jma,kma->jk", regrouped, regrouped, precision=HIGH)
    gram_two = lax.psum(block_second, ("grp", "slab"))
    basis_two = iterate_basis(gram_two, start_two)
    second_rows = tensor.shape[0]
    own_basis = lax.dynamic_slice_in_dim(
        basis_two, lax.axis_index("grp") * second_rows, second_rows, 0
    )
    partial_core = jnp.einsum("jb,jma->bma", own_basis, reduced, precision=HIGH)
    core = lax.psum_scatter(partial_core, "grp", scatter_dimension=0, tiled=True)
    return (basis_one, basis_two, core)


def solution(mesh):
    in_specs = (P("grp", "slab", None), P(), P())
    out_specs = (P(), P(), P("grp", "slab", None))
    return jax.shard_map(local, mesh=mesh, in_specs=in_specs, out_specs=out_specs, check_vma=False)
```

profile of v0, /device:TPU:0, one launch (start us, length us, event | category | flops | bytes accessed | tf_op | source)
XLA Modules:
  0.0 465.3 jit_solution(15145513758969465968)
XLA Ops:
  7.2 18.1 %fusion.4 = f32[672,672]{1,0:T(8,128)} fusion(f32[168,8,672]{2,1,0:T(8,128)} %param.6), kind=kOutput, calls=%fused_computation.5 | convolution fusion | flops 7283146752 | bytes 5419008 | tf_op jit(solution)/shard_map/jmi,jmk->ik/dot_general | solution.py:26
  25.6 152.5 %all-reduce.3.cloned.1.call-done = f32[672,672]{1,0:T(8,128)} async-done(((f32[672,672]{1,0:T(8,128)}), f32[672,672]{1,0:T(8,128)}) %all-reduce.3.cloned.1.call-update) | async-done | bytes 1806352 | tf_op jit(solution)/shard_map/psum | solution.py:27
  178.1 3.7 fusion.30
  182.3 8.8 %cholesky.74 = f32[96,96]{1,0:T(8,128)S(1)} custom-call(f32[96,96]{1,0:T(8,128)S(1)} %fusion.26), custom_call_target="Cholesky" | custom-call | tf_op jit(solution)/shard_map/jit(cholesky)/cholesky | solution.py:12
  191.1 0.6 compare_reduce_fusion.3
  191.7 0.7 fusion.14
  192.4 7.4 %custom-call.8 = f32[1,96,96]{1,2,0:T(8,128)S(1)} custom-call(f32[1,96,96]{2,1,0:T(8,128)S(1)} %fusion.14), custom_call_target="InvertDiagBlocksLowerTriangular" | custom-call | tf_op jit(solution)/shard_map/triangular_solve/custom-call.0 | solution.py:13
  199.8 0.4 convolution_bitcast_fusion.3
  200.2 2.0 fusion.32
  202.7 8.8 %cholesky.85 = f32[96,96]{1,0:T(8,128)S(1)} custom-call(f32[96,96]{1,0:T(8,128)S(1)} %fusion.24), custom_call_target="Cholesky" | custom-call | tf_op jit(solution)/shard_map/jit(cholesky)/cholesky | solution.py:12
  211.5 0.6 compare_reduce_fusion.2
  212.1 0.7 fusion.15
  212.8 7.4 %custom-call.9 = f32[1,96,96]{1,2,0:T(8,128)S(1)} custom-call(f32[1,96,96]{2,1,0:T(8,128)S(1)} %fusion.15), custom_call_target="InvertDiagBlocksLowerTriangular" | custom-call | tf_op jit(solution)/shard_map/triangular_solve/custom-call.0 | solution.py:13
  220.6 6.5 %fusion.7 = f32[168,8,96]{2,0,1:T(8,128)S(1)} fusion(f32[168,8,672]{2,1,0:T(8,128)} %param.6, f32[96,672]{1,0:T(8,128)S(1)} %fusion.22), kind=kOutput, calls=%fused_computation.6 | convolution fusion | flops 1040449536 | bytes 4386816 | tf_op jit(solution)/shard_map/jmi,ia->jma/dot_general | solution.py:29
  227.1 15.1 %all_to_all.18 = f32[168,8,96]{2,0,1:T(8,128)S(1)} all-to-all(f32[168,8,96]{2,0,1:T(8,128)S(1)} %fusion.7), channel_id=1, replica_groups=mesh['grp'=4,'slab'=32] {'grp'}, dimensions={1} | all-to-all | bytes 1032192 | tf_op jit(solution)/shard_map/all_to_all | solution.py:30
  242.2 3.1 convolution_bitcast_fusion
  245.4 147.7 %all-reduce.5.cloned.1.call-done = f32[672,672]{1,0:T(8,128)} async-done(((f32[672,672]{1,0:T(8,128)}), f32[672,672]{1,0:T(8,128)}) %all-reduce.5.cloned.1.call-update) | async-done | bytes 1806352 | tf_op jit(solution)/shard_map/psum | solution.py:32
  393.1 3.7 fusion.34
  397.3 8.8 %cholesky.96 = f32[96,96]{1,0:T(8,128)S(1)} custom-call(f32[96,96]{1,0:T(8,128)S(1)} %fusion.21), custom_call_target="Cholesky" | custom-call | tf_op jit(solution)/shard_map/jit(cholesky)/cholesky | solution.py:12
  406.1 0.6 compare_reduce_fusion.1
  406.7 0.7 fusion.16
  407.4 7.4 %custom-call.10 = f32[1,96,96]{1,2,0:T(8,128)S(1)} custom-call(f32[1,96,96]{2,1,0:T(8,128)S(1)} %fusion.16), custom_call_target="InvertDiagBlocksLowerTriangular" | custom-call | tf_op jit(solution)/shard_map/triangular_solve/custom-call.0 | solution.py:13
  414.8 0.4 convolution_bitcast_fusion.2
  415.2 2.0 fusion.36
  417.7 8.8 %cholesky.107 = f32[96,96]{1,0:T(8,128)S(1)} custom-call(f32[96,96]{1,0:T(8,128)S(1)} %fusion.19), custom_call_target="Cholesky" | custom-call | tf_op jit(solution)/shard_map/jit(cholesky)/cholesky | solution.py:12
  426.5 0.6 compare_reduce_fusion
  427.2 0.7 fusion.17
  427.8 7.4 %custom-call.11 = f32[1,96,96]{1,2,0:T(8,128)S(1)} custom-call(f32[1,96,96]{2,1,0:T(8,128)S(1)} %fusion.17), custom_call_target="InvertDiagBlocksLowerTriangular" | custom-call | tf_op jit(solution)/shard_map/triangular_solve/custom-call.0 | solution.py:13
  435.2 0.4 convolution_bitcast_fusion.1
  435.7 1.3 fusion.11
  437.0 19.9 %reduce-scatter.2.cloned.1.call-done = f32[24,8,96]{2,0,1:T(8,128)} async-done(((f32[96,8,96]{2,0,1:T(8,128)}), f32[24,8,96]{2,0,1:T(8,128)}) %reduce-scatter.2.cloned.1.call-update) | async-done | bytes 73744 | tf_op jit(solution)/shard_map/reduce_scatter | solution.py:39
  456.8 1.6 copy.27
  (34 shorter events, 2.9 us)
Async XLA Ops:
  7.2 170.9 %copy-start = (f32[672,96]{0,1:T(8,128)S(1)}, f32[672,96]{0,1:T(8,128)}, u32[]{:S(2)}) copy-start(f32[672,96]{0,1:T(8,128)} %param.7) | copy-start | bytes 774148
  7.2 170.9 %all-reduce.3.cloned.1.call-start = ((), (), s32[]{:S(2)}) async-start(), calls=%async_computation.2 | async-start | bytes 4128768 | tf_op jit(solution)/shard_map/psum | solution.py:27
  25.3 367.8 %all-reduce.5.cloned.1.call-start = ((), (), s32[]{:S(2)}) async-start(), calls=%async_computation.3 | async-start | bytes 4128768 | tf_op jit(solution)/shard_map/psum | solution.py:32
  178.1 22.1 %copy-start.2 = (f32[672,672]{1,0:T(8,128)S(1)}, f32[672,672]{1,0:T(8,128)}, u32[]{:S(2)}) copy-start(f32[672,672]{1,0:T(8,128)} %all-reduce.3.cloned.1.call-done) | copy-start | bytes 5419012
  220.6 6.5 %copy-start.3 = (f32[96,672]{1,0:T(8,128)}, f32[96,672]{1,0:T(8,128)S(1)}, u32[]{:S(2)}) copy-start(f32[96,672]{1,0:T(8,128)S(1)} %fusion.22) | copy-start | bytes 774148
  245.3 211.5 %reduce-scatter.2.cloned.1.call-start = ((), (), s32[]{:S(2)}) async-start(), calls=%async_computation.4 | async-start | bytes 491520 | tf_op jit(solution)/shard_map/reduce_scatter | solution.py:39
  393.1 22.1 %copy-start.1 = (f32[672,672]{1,0:T(8,128)S(1)}, f32[672,672]{1,0:T(8,128)}, u32[]{:S(2)}) copy-start(f32[672,672]{1,0:T(8,128)} %all-reduce.5.cloned.1.call-done) | copy-start | bytes 5419012
  435.6 22.8 %copy-start.4 = (f32[672,96]{0,1:T(8,128)}, f32[672,96]{0,1:T(8,128)S(1)}, u32[]{:S(2)}) copy-start(f32[672,96]{0,1:T(8,128)S(1)} %convolution_bitcast_fusion.1) | copy-start | bytes 774148
Sparse Core Ops, SparseCore 0:
  25.5 152.5 all-reduce.2
  245.4 147.5 all-reduce.4
  437.1 19.7 reduce-scatter.1
where the time goes:
time: 471 us; the launch traced here: 465 us
  waiting for transfers between devices  320 us (68%)
  other arithmetic  69.9 us (15%)
  matrix products  43.5 us (9%)
  blocking collectives  15.1 us (3%)
  between operations  14.4 us (3%)
    psum x1, waiting for transfers between devices, local(): gram_one = lax.psum(block_gram, ('grp', 'slab'))  153 us
    psum x1, waiting for transfers between devices, local(): gram_two = lax.psum(block_second, ('grp', 'slab'))  148 us
    another operation x12, other arithmetic, orthonormal(): lower_small = jnp.linalg.cholesky(cross)  37.8 us
    another operation x8, other arithmetic, orthonormal(): lax.linalg.triangular_solve(lower_small, widened, left_side=False, lower=...  32 us
    reduce_scatter x1, waiting for transfers between devices, local(): lax.psum_scatter(partial_core, 'grp', scatter_dimension=0, tiled=True)  19.9 us
    dot_general x1, matrix products, local(): block_gram = jnp.einsum('jmi,jmk->ik', tensor, tensor, precision=HIGH)  18.1 us
    all_to_all x1, blocking collectives, local(): lax.all_to_all(reduced, 'grp', split_axis=1, concat_axis=0, tiled=True)  15.1 us
    dot_general x4, matrix products, iterate_basis(): current = orthonormal(jnp.dot(gram, current, precision=HIGH))  11.3 us
  transfers between devices with their start and end apart: 3, of which 3 were waited for; matrix products, arithmetic and copies ran while one was open for 0% of the time, Pallas kernels for 0%

commit v1 on v0

--- a/solution.py
+++ b/solution.py
@@ -29,7 +29,9 @@
     reduced = jnp.einsum("jmi,ia->jma", tensor, basis_one, precision=HIGH)
     regrouped = lax.all_to_all(reduced, "grp", split_axis=1, concat_axis=0, tiled=True)
     block_second = jnp.einsum("jma,kma->jk", regrouped, regrouped, precision=HIGH)
-    gram_two = lax.psum(block_second, ("grp", "slab"))
+    gram_two = block_second
+    for axis in ("slab", "grp"):
+        gram_two = lax.psum(gram_two, axis)
     basis_two = iterate_basis(gram_two, start_two)
     second_rows = tensor.shape[0]
     own_basis = lax.dynamic_slice_in_dim(

time: 471 us -> 490 us (1.040)
  waiting for transfers between devices: 320 us -> 339 us
    psum x1 -> x2, waiting for transfers between devices: 148 us -> 165 us  [local(): gram_two = lax.psum(gram_two, axis)]
  transfers between devices with their start and end apart: 3 -> 4, of which waited for: 3 -> 4; matrix products, arithmetic and copies ran while one was open for 0% -> 0% of each run, Pallas kernels for 0% -> 0%
where the time goes in v1:
time: 490 us; the launch traced here: 484 us
  waiting for transfers between devices  339 us (69%)
  other arithmetic  69.9 us (14%)
  matrix products  43.6 us (9%)
  blocking collectives  15.1 us (3%)
  between operations  14.4 us (3%)
    psum x2, waiting for transfers between devices, local(): gram_two = lax.psum(gram_two, axis)  165 us
    psum x1, waiting for transfers between devices, local(): gram_one = lax.psum(block_gram, ('grp', 'slab'))  153 us
    another operation x12, other arithmetic, orthonormal(): lower_small = jnp.linalg.cholesky(cross)  37.8 us
    another operation x8, other arithmetic, orthonormal(): lax.linalg.triangular_solve(lower_small, widened, left_side=False, lower=...  32 us
    reduce_scatter x1, waiting for transfers between devices, local(): lax.psum_scatter(partial_core, 'grp', scatter_dimension=0, tiled=True)  21 us
    dot_general x1, matrix products, local(): block_gram = jnp.einsum('jmi,jmk->ik', tensor, tensor, precision=HIGH)  18.1 us
    all_to_all x1, blocking collectives, local(): lax.all_to_all(reduced, 'grp', split_axis=1, concat_axis=0, tiled=True)  15.1 us
    dot_general x4, matrix products, iterate_basis(): current = orthonormal(jnp.dot(gram, current, precision=HIGH))  11.3 us
  transfers between devices with their start and end apart: 4, of which 4 were waited for; matrix products, arithmetic and copies ran while one was open for 0% of the time, Pallas kernels for 0%

profile of v1, /device:TPU:0, one launch (start us, length us, event | category | flops | bytes accessed | tf_op | source)
XLA Modules:
  0.0 484.2 jit_solution(2123889477987052942)
XLA Ops:
  7.2 18.1 %fusion.4 = f32[672,672]{1,0:T(8,128)} fusion(f32[168,8,672]{2,1,0:T(8,128)} %param.6), kind=kOutput, calls=%fused_computation.5 | convolution fusion | flops 7283146752 | bytes 5419008 | tf_op jit(solution)/shard_map/jmi,jmk->ik/dot_general | solution.py:26
  25.6 152.5 %all-reduce.4.cloned.1.call-done = f32[672,672]{1,0:T(8,128)} async-done(((f32[672,672]{1,0:T(8,128)}), f32[672,672]{1,0:T(8,128)}) %all-reduce.4.cloned.1.call-update) | async-done | bytes 1806352 | tf_op jit(solution)/shard_map/psum | solution.py:27
  178.1 3.7 fusion.30
  182.3 8.8 %cholesky.74 = f32[96,96]{1,0:T(8,128)S(1)} custom-call(f32[96,96]{1,0:T(8,128)S(1)} %fusion.26), custom_call_target="Cholesky" | custom-call | tf_op jit(solution)/shard_map/jit(cholesky)/cholesky | solution.py:12
  191.1 0.6 compare_reduce_fusion.3
  191.7 0.7 fusion.14
  192.4 7.4 %custom-call.8 = f32[1,96,96]{1,2,0:T(8,128)S(1)} custom-call(f32[1,96,96]{2,1,0:T(8,128)S(1)} %fusion.14), custom_call_target="InvertDiagBlocksLowerTriangular" | custom-call | tf_op jit(solution)/shard_map/triangular_solve/custom-call.0 | solution.py:13
  199.8 0.4 convolution_bitcast_fusion.3
  200.2 2.0 fusion.32
  202.7 8.8 %cholesky.85 = f32[96,96]{1,0:T(8,128)S(1)} custom-call(f32[96,96]{1,0:T(8,128)S(1)} %fusion.24), custom_call_target="Cholesky" | custom-call | tf_op jit(solution)/shard_map/jit(cholesky)/cholesky | solution.py:12
  211.5 0.6 compare_reduce_fusion.2
  212.1 0.7 fusion.15
  212.8 7.4 %custom-call.9 = f32[1,96,96]{1,2,0:T(8,128)S(1)} custom-call(f32[1,96,96]{2,1,0:T(8,128)S(1)} %fusion.15), custom_call_target="InvertDiagBlocksLowerTriangular" | custom-call | tf_op jit(solution)/shard_map/triangular_solve/custom-call.0 | solution.py:13
  220.2 0.4 fusion.22
  220.6 6.5 %fusion.7 = f32[168,8,96]{2,0,1:T(8,128)S(1)} fusion(f32[168,8,672]{2,1,0:T(8,128)} %param.6, f32[96,672]{1,0:T(8,128)S(1)} %fusion.22), kind=kOutput, calls=%fused_computation.6 | convolution fusion | flops 1040449536 | bytes 4386816 | tf_op jit(solution)/shard_map/jmi,ia->jma/dot_general | solution.py:29
  227.1 15.1 %all_to_all.18 = f32[168,8,96]{2,0,1:T(8,128)S(1)} all-to-all(f32[168,8,96]{2,0,1:T(8,128)S(1)} %fusion.7), channel_id=1, replica_groups=mesh['grp'=4,'slab'=32] {'grp'}, dimensions={1} | all-to-all | bytes 1032192 | tf_op jit(solution)/shard_map/all_to_all | solution.py:30
  242.2 3.1 convolution_bitcast_fusion
  245.4 104.9 %all-reduce.6.cloned.1.call-done = f32[672,672]{1,0:T(8,128)} async-done(((f32[672,672]{1,0:T(8,128)}), f32[672,672]{1,0:T(8,128)}) %all-reduce.6.cloned.1.call-update) | async-done | bytes 1806352 | tf_op jit(solution)/shard_map/psum | solution.py:34
  350.3 60.5 %all-reduce.8.cloned.1.call-done = f32[672,672]{1,0:T(8,128)} async-done(((f32[672,672]{1,0:T(8,128)}), f32[672,672]{1,0:T(8,128)}) %all-reduce.8.cloned.1.call-update) | async-done | bytes 1806352 | tf_op jit(solution)/shard_map/psum | solution.py:34
  410.8 3.7 fusion.34
  415.0 8.8 %cholesky.96 = f32[96,96]{1,0:T(8,128)S(1)} custom-call(f32[96,96]{1,0:T(8,128)S(1)} %fusion.21), custom_call_target="Cholesky" | custom-call | tf_op jit(solution)/shard_map/jit(cholesky)/cholesky | solution.py:12
  423.9 0.6 compare_reduce_fusion.1
  424.5 0.7 fusion.16
  425.2 7.4 %custom-call.10 = f32[1,96,96]{1,2,0:T(8,128)S(1)} custom-call(f32[1,96,96]{2,1,0:T(8,128)S(1)} %fusion.16), custom_call_target="InvertDiagBlocksLowerTriangular" | custom-call | tf_op jit(solution)/shard_map/triangular_solve/custom-call.0 | solution.py:13
  433.0 2.0 fusion.36
  435.5 8.8 %cholesky.107 = f32[96,96]{1,0:T(8,128)S(1)} custom-call(f32[96,96]{1,0:T(8,128)S(1)} %fusion.19), custom_call_target="Cholesky" | custom-call | tf_op jit(solution)/shard_map/jit(cholesky)/cholesky | solution.py:12
  444.3 0.6 compare_reduce_fusion
  444.9 0.7 fusion.17
  445.6 7.4 %custom-call.11 = f32[1,96,96]{1,2,0:T(8,128)S(1)} custom-call(f32[1,96,96]{2,1,0:T(8,128)S(1)} %fusion.17), custom_call_target="InvertDiagBlocksLowerTriangular" | custom-call | tf_op jit(solution)/shard_map/triangular_solve/custom-call.0 | solution.py:13
  453.4 1.3 fusion.11
  454.7 21.0 %reduce-scatter.2.cloned.1.call-done = f32[24,8,96]{2,0,1:T(8,128)} async-done(((f32[96,8,96]{2,0,1:T(8,128)}), f32[24,8,96]{2,0,1:T(8,128)}) %reduce-scatter.2.cloned.1.call-update) | async-done | bytes 73744 | tf_op jit(solution)/shard_map/reduce_scatter | solution.py:41
  475.7 1.6 copy.27
  (37 shorter events, 3.4 us)
Async XLA Ops:
  7.2 170.9 %copy-start = (f32[672,96]{0,1:T(8,128)S(1)}, f32[672,96]{0,1:T(8,128)}, u32[]{:S(2)}) copy-start(f32[672,96]{0,1:T(8,128)} %param.7) | copy-start | bytes 774148
  7.2 170.9 %all-reduce.4.cloned.1.call-start = ((), (), s32[]{:S(2)}) async-start(), calls=%async_computation.2 | async-start | bytes 4128768 | tf_op jit(solution)/shard_map/psum | solution.py:27
  25.3 324.9 %all-reduce.6.cloned.1.call-start = ((), (), s32[]{:S(2)}) async-start(), calls=%async_computation.3 | async-start | bytes 4128768 | tf_op jit(solution)/shard_map/psum | solution.py:34
  178.1 22.1 %copy-start.2 = (f32[672,672]{1,0:T(8,128)S(1)}, f32[672,672]{1,0:T(8,128)}, u32[]{:S(2)}) copy-start(f32[672,672]{1,0:T(8,128)} %all-reduce.4.cloned.1.call-done) | copy-start | bytes 5419012
  220.6 6.5 %copy-start.3 = (f32[96,672]{1,0:T(8,128)}, f32[96,672]{1,0:T(8,128)S(1)}, u32[]{:S(2)}) copy-start(f32[96,672]{1,0:T(8,128)S(1)} %fusion.22) | copy-start | bytes 774148
  245.3 165.5 %all-reduce.8.cloned.1.call-start = ((), (), s32[]{:S(2)}) async-start(), calls=%async_computation.4 | async-start | bytes 4128768 | tf_op jit(solution)/shard_map/psum | solution.py:34
  350.3 125.4 %reduce-scatter.2.cloned.1.call-start = ((), (), s32[]{:S(2)}) async-start(), calls=%async_computation.5 | async-start | bytes 491520 | tf_op jit(solution)/shard_map/reduce_scatter | solution.py:41
  410.8 22.1 %copy-start.1 = (f32[672,672]{1,0:T(8,128)S(1)}, f32[672,672]{1,0:T(8,128)}, u32[]{:S(2)}) copy-start(f32[672,672]{1,0:T(8,128)} %all-reduce.8.cloned.1.call-done) | copy-start | bytes 5419012
  453.4 23.9 %copy-start.4 = (f32[672,96]{0,1:T(8,128)}, f32[672,96]{0,1:T(8,128)S(1)}, u32[]{:S(2)}) copy-start(f32[672,96]{0,1:T(8,128)S(1)} %convolution_bitcast_fusion.1) | copy-start | bytes 774148
Sparse Core Ops, SparseCore 0:
  25.5 152.5 all-reduce.3
  245.5 104.7 all-reduce.5
  352.6 58.1 all-reduce.7
  454.8 20.8 reduce-scatter.1
